TPU v7x, 512 devices: a whole 4x8x8 slice. The times are simulated.
512 devices in a mesh: rows: 32 (over z_lo, y), cols: 16 (over x, z_hi, core).
Axes of the slice: x: 4, y: 8, z: 8 (z_hi: 2, z_lo: 4; z = z_hi * 4 + z_lo), core: 2. Of those that a mesh axis runs over, the one named last changes fastest.
Arguments:
- series: float32 [2097152], P(('rows', 'cols')), may hold values from -6 to 6
- tile_list: int32 [3, 2048], P(None, 'rows'), may hold values from 0 to 4094, as said below
Outputs:
- profile: float32 [2097152], P(('rows', 'cols'))
Inputs may be any that keep to these rules, and one draw needn't show every extreme that they name: The columns of tile_list lying on one index of rows list 64 distinct tiles (row block, offset) of that row group: the row block lies in the group, the offset is below 8, and row block plus offset is at most 4094. Every group but the last lists a tile whose column block lies in the next group; the last group lists the tile of row block 4094 and offset 0. The third row is an index of cols; in each group no index owns more than 8 tiles and one owns exactly 8.
All inputs are finite; a program needn't handle non-finite values.
Results may differ from a plain program's by a relative error of at most 0.0001.
Values sent between devices are 32-bit elements; how exact they have to be, the bound alone decides.
A program may use at most 64 MiB of HBM per device.

v0:
```python
import math
import jax
import jax.numpy as jnp
from jax import lax
from jax.sharding import PartitionSpec as P

M = 256
B = 512
BPR = 128
CAP = 8
NEXT = 4096
EXCL = 64


def passed_along(block, axis, distance):
    devices = range(lax.axis_size(axis))
    route = [(i - distance, i) for i in devices if i - distance in devices]
    return lax.ppermute(block, axis, route)


def hankel(values, rows, width):
    length = values.shape[0]
    flat = jnp.concatenate([jnp.tile(values, rows), jnp.zeros((rows,), values.dtype)])
    return flat.reshape(rows, length + 1)[:, :width]


def normalize(values):
    windows = hankel(values, B, M)
    centre = windows - jnp.mean(windows, axis=1, keepdims=True)
    spread = jnp.mean(centre * centre, axis=1)
    factor = lax.rsqrt(spread + 1e-05) / math.sqrt(M)
    return centre * factor[:, None]


def tile_maxima(left_data, right_data, offset):
    left_z = normalize(left_data)
    right_z = normalize(right_data)
    corr = lax.dot_general(
        left_z,
        right_z,
        (((1,), (1,)), ((), ())),
        precision=lax.Precision.HIGHEST,
        preferred_element_type=jnp.float32,
    )
    row_pos = lax.broadcasted_iota(jnp.int32, (B, B), 0)
    col_pos = lax.broadcasted_iota(jnp.int32, (B, B), 1)
    keep = offset * B + col_pos - row_pos >= EXCL
    corr = jnp.where(keep, corr, jnp.float32(-1.0))
    return (jnp.max(corr, axis=1), jnp.max(corr, axis=0))


def raise_block(partial_max, start, values):
    current = lax.dynamic_slice_in_dim(partial_max, start, B)
    return lax.dynamic_update_slice_in_dim(partial_max, jnp.maximum(current, values), start, 0)


def on_device(series, tile_list):
    piece = series.shape[0]
    col_count = lax.axis_size("cols")
    seg_len = piece * col_count
    group = lax.axis_index("rows")
    col_id = lax.axis_index("cols")
    segment = lax.all_gather(series, "cols", axis=0, tiled=True)
    head = passed_along(segment[:NEXT], "rows", -1)
    signal = jnp.concatenate([segment, head])
    foreign = (tile_list[2] != col_id).astype(jnp.int32)
    order = jnp.argsort(foreign, stable=True)[:CAP]
    live = tile_list[2][order] == col_id
    slots = CAP
    partial_max = jnp.full((seg_len + NEXT,), -1.0, jnp.float32)

    def step(index, partial_max):
        which = order[index]
        local_block = tile_list[0, which] - group * BPR
        offset = tile_list[1, which]
        row_start = local_block * B
        col_start = (local_block + offset) * B
        left_data = lax.dynamic_slice_in_dim(signal, row_start, B + M)
        right_data = lax.dynamic_slice_in_dim(signal, col_start, B + M)
        row_max, col_max = tile_maxima(left_data, right_data, offset)
        active = live[index]
        row_max = jnp.where(active, row_max, jnp.float32(-1.0))
        col_max = jnp.where(active, col_max, jnp.float32(-1.0))
        partial_max = raise_block(partial_max, row_start, row_max)
        return raise_block(partial_max, col_start, col_max)

    partial_max = lax.fori_loop(0, slots, step, partial_max)
    own_part = partial_max[:seg_len]
    spill = partial_max[seg_len:]
    own_part, spill = lax.pmax((own_part, spill), "cols")
    arrived = passed_along(spill, "rows", 1)
    arrived = jnp.where(group > 0, arrived, jnp.float32(-1.0))
    own_part = jnp.concatenate([jnp.maximum(own_part[:NEXT], arrived), own_part[NEXT:]])
    return lax.dynamic_slice_in_dim(own_part, col_id * piece, piece)


def solution(mesh):
    in_specs = (P(("rows", "cols")), P(None, "rows"))
    out_specs = P(("rows", "cols"))
    return jax.shard_map(
        on_device, mesh=mesh, in_specs=in_specs, out_specs=out_specs, check_vma=False
    )
```

profile of v0, /device:TPU:1, one launch (start us, length us, event | category | flops | bytes accessed | tf_op | source)
XLA Modules:
  0.0 393.8 jit_solution(1997206631718759267)
XLA Ops:
  6.5 37.6 %all_gather.3 = f32[65536]{0:T(1024)S(1)} all-gather(f32[4096]{0:T(1024)} %param.4), channel_id=1, replica_groups=mesh['rows'=32,'cols'=16] {'cols'}, dimensions={0}, use_global_device_ids=true | all-gather | bytes 278528 | tf_op jit(solution)/shard_map/all_gather | solution.py:63
  46.8 2.0 sort.17
  50.3 152.8 %while.15 = (s32[]{:T(128)}, f32[69632]{0:T(1024)}, s32[8]{0:T(128)S(1)}, s32[3,64]{1,0:T(4,128)}, s32[]{:T(128)}, /*index=5*/pred[8]{0:T(512)(128)(4,1)S(1)}, f...) while((s32[]{:T(128)}, f32[69632]{0:T(1024)}, ...), condition=%wide.region_8.9_spmd, body=%wide.region_1.8_spmd.sunk | while | flops 808193536 | bytes 33783220 | solution.py:87
  53.0 1.4 constant_dynamic-slice_fusion.3
  56.1 1.6 reshape.64
  59.3 1.6 reshape.63
  61.9 2.4 fusion.12
  65.0 2.2 maximum_dynamic-update-slice_fusion.4
  67.2 2.2 maximum_dynamic-update-slice_fusion.5
  75.2 1.6 reshape.64
  78.4 1.6 reshape.63
  81.0 2.4 fusion.12
  84.1 2.2 maximum_dynamic-update-slice_fusion.4
  86.3 2.2 maximum_dynamic-update-slice_fusion.5
  94.3 1.6 reshape.64
  97.5 1.6 reshape.63
  100.1 2.4 fusion.12
  103.1 2.2 maximum_dynamic-update-slice_fusion.4
  105.3 2.2 maximum_dynamic-update-slice_fusion.5
  113.4 1.6 reshape.64
  116.6 1.6 reshape.63
  119.2 2.4 fusion.12
  122.2 2.2 maximum_dynamic-update-slice_fusion.4
  124.4 2.2 maximum_dynamic-update-slice_fusion.5
  132.5 1.6 reshape.64
  135.7 1.6 reshape.63
  138.3 2.4 fusion.12
  141.3 2.2 maximum_dynamic-update-slice_fusion.4
  143.5 2.2 maximum_dynamic-update-slice_fusion.5
  151.6 1.6 reshape.64
  154.8 1.6 reshape.63
  157.4 2.4 fusion.12
  160.4 2.2 maximum_dynamic-update-slice_fusion.4
  162.6 2.2 maximum_dynamic-update-slice_fusion.5
  170.7 1.6 reshape.64
  173.9 1.6 reshape.63
  176.5 2.4 fusion.12
  179.5 2.2 maximum_dynamic-update-slice_fusion.4
  181.8 2.2 maximum_dynamic-update-slice_fusion.5
  189.8 1.6 reshape.64
  193.0 1.6 reshape.63
  195.6 2.4 fusion.12
  198.7 2.2 maximum_dynamic-update-slice_fusion.4
  200.9 2.2 maximum_dynamic-update-slice_fusion.5
  203.1 1.7 slice.43
  205.5 76.3 %pmax.15 = f32[4096]{0:T(1024)S(1)} all-reduce(f32[4096]{0:T(1024)S(1)} %slice.45), channel_id=1, replica_groups=mesh['rows'=32,'cols'=16] {'cols'}, use_global_device_ids=true, to_apply=%region_10.11 | all-reduce | flops 4096 | bytes 32768 | tf_op jit(solution)/shard_map/pmax | solution.py:90
  281.8 4.0 %collective-permute-start.1 = (f32[4096]{0:T(1024)S(1)}, f32[4096]{0:T(1024)S(1)}, u32[]{:S(2)}, u32[]{:S(2)}) collective-permute-start(f32[4096]{0:T(1024)S(1)} %pmax.15), channel_id=1, source_target_pairs={{0,16},{16,32},{32,48},{48,64},{64,80},{80,96},{96,112},{112,128},... | collective-permute-start | bytes 49160 | tf_op jit(solution)/shard_map/ppermute | solution.py:18
  285.8 98.8 %all-reduce.4.cloned.1.call-done = f32[65536]{0:T(1024)} async-done(((f32[65536]{0:T(1024)}), f32[65536]{0:T(1024)}) %all-reduce.4.cloned.1.call-update) | async-done | bytes 262160 | tf_op jit(solution)/shard_map/pmax | solution.py:90
  (210 shorter events, 46.7 us)
Async XLA Ops:
  6.5 378.1 %all-reduce.4.cloned.1.call-start = ((), (), s32[]{:S(2)}) async-start(), calls=%async_computation | async-start | bytes 524288 | tf_op jit(solution)/shard_map/pmax | solution.py:90
  44.1 5.4 %collective-permute-start = (f32[4096]{0:T(1024)S(1)}, f32[4096]{0:T(1024)S(1)}, u32[]{:S(2)}, u32[]{:S(2)}) collective-permute-start(f32[4096]{0:T(1024)S(1)} %slice.51), channel_id=1, source_target_pairs={{16,0},{32,16},{48,32},{64,48},{80,64},{96,80},{112,96},{128,112},... | collective-permute-start | bytes 49160 | tf_op jit(solution)/shard_map/ppermute | solution.py:18
  50.3 5.5 %copy-start.1 = (f32[69632]{0:T(1024)}, f32[69632]{0:T(1024)S(1)}, u32[]{:S(2)}) copy-start(f32[69632]{0:T(1024)S(1)} %get-tuple-element.293) | copy-start | bytes 835588 | tf_op jit(solution)/shard_map/while
  57.7 1.3 copy-start
  60.9 8.5 %copy-start.2 = (f32[69632]{0:T(1024)S(1)}, f32[69632]{0:T(1024)}, u32[]{:S(2)}) copy-start(f32[69632]{0:T(1024)} %copy-done.1) | copy-start | bytes 835588 | tf_op jit(solution)/shard_map/while
  69.4 5.5 %copy-start.1 = (f32[69632]{0:T(1024)}, f32[69632]{0:T(1024)S(1)}, u32[]{:S(2)}) copy-start(f32[69632]{0:T(1024)S(1)} %get-tuple-element.293) | copy-start | bytes 835588 | tf_op jit(solution)/shard_map/while
  76.8 1.3 copy-start
  80.0 8.5 %copy-start.2 = (f32[69632]{0:T(1024)S(1)}, f32[69632]{0:T(1024)}, u32[]{:S(2)}) copy-start(f32[69632]{0:T(1024)} %copy-done.1) | copy-start | bytes 835588 | tf_op jit(solution)/shard_map/while
  88.5 5.5 %copy-start.1 = (f32[69632]{0:T(1024)}, f32[69632]{0:T(1024)S(1)}, u32[]{:S(2)}) copy-start(f32[69632]{0:T(1024)S(1)} %get-tuple-element.293) | copy-start | bytes 835588 | tf_op jit(solution)/shard_map/while
  95.9 1.3 copy-start
  99.1 8.5 %copy-start.2 = (f32[69632]{0:T(1024)S(1)}, f32[69632]{0:T(1024)}, u32[]{:S(2)}) copy-start(f32[69632]{0:T(1024)} %copy-done.1) | copy-start | bytes 835588 | tf_op jit(solution)/shard_map/while
  107.5 5.5 %copy-start.1 = (f32[69632]{0:T(1024)}, f32[69632]{0:T(1024)S(1)}, u32[]{:S(2)}) copy-start(f32[69632]{0:T(1024)S(1)} %get-tuple-element.293) | copy-start | bytes 835588 | tf_op jit(solution)/shard_map/while
  115.0 1.3 copy-start
  118.2 8.5 %copy-start.2 = (f32[69632]{0:T(1024)S(1)}, f32[69632]{0:T(1024)}, u32[]{:S(2)}) copy-start(f32[69632]{0:T(1024)} %copy-done.1) | copy-start | bytes 835588 | tf_op jit(solution)/shard_map/while
  126.6 5.5 %copy-start.1 = (f32[69632]{0:T(1024)}, f32[69632]{0:T(1024)S(1)}, u32[]{:S(2)}) copy-start(f32[69632]{0:T(1024)S(1)} %get-tuple-element.293) | copy-start | bytes 835588 | tf_op jit(solution)/shard_map/while
  134.1 1.3 copy-start
  137.3 8.5 %copy-start.2 = (f32[69632]{0:T(1024)S(1)}, f32[69632]{0:T(1024)}, u32[]{:S(2)}) copy-start(f32[69632]{0:T(1024)} %copy-done.1) | copy-start | bytes 835588 | tf_op jit(solution)/shard_map/while
  145.8 5.5 %copy-start.1 = (f32[69632]{0:T(1024)}, f32[69632]{0:T(1024)S(1)}, u32[]{:S(2)}) copy-start(f32[69632]{0:T(1024)S(1)} %get-tuple-element.293) | copy-start | bytes 835588 | tf_op jit(solution)/shard_map/while
  153.2 1.3 copy-start
  156.4 8.5 %copy-start.2 = (f32[69632]{0:T(1024)S(1)}, f32[69632]{0:T(1024)}, u32[]{:S(2)}) copy-start(f32[69632]{0:T(1024)} %copy-done.1) | copy-start | bytes 835588 | tf_op jit(solution)/shard_map/while
  164.8 5.5 %copy-start.1 = (f32[69632]{0:T(1024)}, f32[69632]{0:T(1024)S(1)}, u32[]{:S(2)}) copy-start(f32[69632]{0:T(1024)S(1)} %get-tuple-element.293) | copy-start | bytes 835588 | tf_op jit(solution)/shard_map/while
  172.3 1.3 copy-start
  175.5 8.5 %copy-start.2 = (f32[69632]{0:T(1024)S(1)}, f32[69632]{0:T(1024)}, u32[]{:S(2)}) copy-start(f32[69632]{0:T(1024)} %copy-done.1) | copy-start | bytes 835588 | tf_op jit(solution)/shard_map/while
  184.0 5.5 %copy-start.1 = (f32[69632]{0:T(1024)}, f32[69632]{0:T(1024)S(1)}, u32[]{:S(2)}) copy-start(f32[69632]{0:T(1024)S(1)} %get-tuple-element.293) | copy-start | bytes 835588 | tf_op jit(solution)/shard_map/while
  191.4 1.3 copy-start
  194.6 8.5 %copy-start.2 = (f32[69632]{0:T(1024)S(1)}, f32[69632]{0:T(1024)}, u32[]{:S(2)}) copy-start(f32[69632]{0:T(1024)} %copy-done.1) | copy-start | bytes 835588 | tf_op jit(solution)/shard_map/while
  281.8 103.8 %collective-permute-start.1 = (f32[4096]{0:T(1024)S(1)}, f32[4096]{0:T(1024)S(1)}, u32[]{:S(2)}, u32[]{:S(2)}) collective-permute-start(f32[4096]{0:T(1024)S(1)} %pmax.15), channel_id=1, source_target_pairs={{0,16},{16,32},{32,48},{48,64},{64,80},{80,96},{96,112},{112,128},... | collective-permute-start | bytes 49160 | tf_op jit(solution)/shard_map/ppermute | solution.py:18
Sparse Core Ops, SparseCore 0:
  204.9 179.7 all-reduce.3
where the time goes:
time: 397 us; the launch traced here: 394 us
  blocking collectives  114 us (29%)
  waiting for transfers between devices  98.9 us (25%)
  local copies, waits for them, and re-layouts  65.3 us (16%)
  other arithmetic  45.5 us (11%)
  loops' own time  32.2 us (8%)
  matrix products  19.2 us (5%)
  between operations  13.5 us (3%)
  starting transfers between devices  5.3 us (1%)
    pmax x1, waiting for transfers between devices, on_device(): own_part, spill = lax.pmax((own_part, spill), 'cols')  98.8 us
    pmax x1, blocking collectives, on_device(): own_part, spill = lax.pmax((own_part, spill), 'cols')  76.3 us
    all_gather x1, blocking collectives, on_device(): segment = lax.all_gather(series, 'cols', axis=0, tiled=True)  37.6 us
    dynamic_update_slice x16, other arithmetic, raise_block(): lax.dynamic_update_slice_in_dim(partial_max, jnp.maximum(current, values)...  35.3 us
    another operation x1, loops' own time, on_device(): partial_max = lax.fori_loop(0, slots, step, partial_max)  32.2 us
    reshape x16, local copies, waits for them, and re-layouts, hankel(): return flat.reshape(rows, length + 1)[:, :width]  25.1 us
    dot_general x8, matrix products, tile_maxima(): lax.dot_general(left_z, right_z, (((1,), (1,)), ((), ())), precision=lax....  19.2 us
    dynamic_slice x8, local copies, waits for them, and re-layouts, step(): offset = tile_list[1, which]  11.4 us
  transfers between devices with their start and end apart: 3, of which 1 were waited for; matrix products, arithmetic and copies ran while one was open for 1% of the time, Pallas kernels for 0%

commit v1 on v0

--- a/solution.py
+++ b/solution.py
@@ -3,6 +3,7 @@
 import jax.numpy as jnp
 from jax import lax
 from jax.sharding import PartitionSpec as P
+from jax.lax import all_to_all, psum
 
 M = 256
 B = 512
@@ -60,7 +61,8 @@
     seg_len = piece * col_count
     group = lax.axis_index("rows")
     col_id = lax.axis_index("cols")
-    segment = lax.all_gather(series, "cols", axis=0, tiled=True)
+    known = all_to_all(jnp.stack([series] * psum(1, "cols")), "cols", concat_axis=0, split_axis=0)
+    segment = jnp.concatenate(known, axis=0)
     head = passed_along(segment[:NEXT], "rows", -1)
     signal = jnp.concatenate([segment, head])
     foreign = (tile_list[2] != col_id).astype(jnp.int32)

time: 397 us -> 382 us (0.962)
  blocking collectives: 114 us -> 78.1 us
  starting transfers between devices: 5.3 us -> 18.8 us
  waiting for transfers between devices: 98.9 us -> 111 us
  local copies, waits for them, and re-layouts: 65.3 us -> 60.9 us
    all_gather x1 -> x0, blocking collectives: 37.6 us -> none  [on_device(): segment = lax.all_gather(series, 'cols', axis=0, tiled=True)]
    all_to_all x0 -> x1, starting transfers between devices: none -> 14.3 us  [on_device(): all_to_all(jnp.stack([series] * psum(1, 'cols')), 'cols', concat_axis=0,...]
    all_to_all x0 -> x1, waiting for transfers between devices: none -> 7.01 us  [on_device(): all_to_all(jnp.stack([series] * psum(1, 'cols')), 'cols', concat_axis=0,...]
    dynamic_slice x8, local copies, waits for them, and re-layouts: 11.4 us -> 5.36 us  [step(): offset = tile_list[1, which]]
  transfers between devices with their start and end apart: 3 -> 4, of which waited for: 1 -> 3; matrix products, arithmetic and copies ran while one was open for 1% -> 2% of each run, Pallas kernels for 0% -> 0%
where the time goes in v1:
time: 382 us; the launch traced here: 379 us
  waiting for transfers between devices  111 us (29%)
  blocking collectives  78.1 us (20%)
  local copies, waits for them, and re-layouts  60.9 us (16%)
  other arithmetic  45.5 us (12%)
  loops' own time  32.2 us (8%)
  matrix products  19.3 us (5%)
  starting transfers between devices  18.8 us (5%)
  between operations  13.5 us (4%)
    pmax x1, waiting for transfers between devices, on_device(): own_part, spill = lax.pmax((own_part, spill), 'cols')  101 us
    pmax x1, blocking collectives, on_device(): own_part, spill = lax.pmax((own_part, spill), 'cols')  78.1 us
    dynamic_update_slice x16, other arithmetic, raise_block(): lax.dynamic_update_slice_in_dim(partial_max, jnp.maximum(current, values)...  35.3 us
    another operation x1, loops' own time, on_device(): partial_max = lax.fori_loop(0, slots, step, partial_max)  32.2 us
    reshape x16, local copies, waits for them, and re-layouts, hankel(): return flat.reshape(rows, length + 1)[:, :width]  25.1 us
    dot_general x8, matrix products, tile_maxima(): lax.dot_general(left_z, right_z, (((1,), (1,)), ((), ())), precision=lax....  19.3 us
    all_to_all x1, starting transfers between devices, on_device(): all_to_all(jnp.stack([series] * psum(1, 'cols')), 'cols', concat_axis=0,...  14.3 us
  transfers between devices with their start and end apart: 4, of which 3 were waited for; matrix products, arithmetic and copies ran while one was open for 2% of the time, Pallas kernels for 0%

profile of v1, /device:TPU:1, one launch (start us, length us, event | category | flops | bytes accessed | tf_op | source)
XLA Modules:
  0.0 379.2 jit_solution(2330170746658820155)
XLA Ops:
  6.5 1.6 stack.2
  8.2 14.3 %all-to-all-start = ((f32[16,1,4096]{2,1,0:T(1,128)}), f32[16,1,4096]{2,1,0:T(1,128)S(1)}, u32[]{:S(2)}, u32[]{:S(2)}) async-start(f32[16,1,4096]{2,1,0:T(1,128)} %stack.2), calls=%async_computation | async-start | bytes 524288 | tf_op jit(solution)/shard_map/all_to_all | solution.py:64
  23.2 2.0 sort.17
  26.5 7.0 %all-to-all-done = f32[16,1,4096]{2,1,0:T(1,128)S(1)} async-done(((f32[16,1,4096]{2,1,0:T(1,128)}), f32[16,1,4096]{2,1,0:T(1,128)S(1)}, u32[]{:S(2)}, u32[]{:S(2)}) %all-to-all-start) | async-done | bytes 262176 | tf_op jit(solution)/shard_map/all_to_all | solution.py:64
  34.9 3.2 collective-permute-done
  38.8 146.8 %while.15 = (s32[]{:T(128)}, f32[69632]{0:T(1024)}, s32[8]{0:T(128)S(1)}, s32[3,64]{1,0:T(4,128)S(1)}, s32[]{:T(128)}, /*index=5*/pred[8]{0:T(512)(128)(4,1)S(1)...) while((s32[]{:T(128)}, f32[69632]{0:T(1024)}, ...), condition=%wide.region_8.9_spmd, body=%wide.region_1.8_spmd.sunk | while | flops 808193536 | bytes 33783220 | solution.py:89
  43.9 1.6 reshape.79
  47.1 1.6 reshape.78
  49.7 2.4 fusion.12
  52.7 2.2 maximum_dynamic-update-slice_fusion.4
  55.0 2.2 maximum_dynamic-update-slice_fusion.5
  62.3 1.6 reshape.79
  65.4 1.6 reshape.78
  68.0 2.4 fusion.12
  71.1 2.2 maximum_dynamic-update-slice_fusion.4
  73.3 2.2 maximum_dynamic-update-slice_fusion.5
  80.6 1.6 reshape.79
  83.8 1.6 reshape.78
  86.4 2.4 fusion.12
  89.4 2.2 maximum_dynamic-update-slice_fusion.4
  91.6 2.2 maximum_dynamic-update-slice_fusion.5
  99.0 1.6 reshape.79
  102.1 1.6 reshape.78
  104.7 2.4 fusion.12
  107.8 2.2 maximum_dynamic-update-slice_fusion.4
  110.0 2.2 maximum_dynamic-update-slice_fusion.5
  117.3 1.6 reshape.79
  120.5 1.6 reshape.78
  123.0 2.4 fusion.12
  126.1 2.2 maximum_dynamic-update-slice_fusion.4
  128.3 2.2 maximum_dynamic-update-slice_fusion.5
  135.7 1.6 reshape.79
  138.8 1.6 reshape.78
  141.4 2.4 fusion.12
  144.5 2.2 maximum_dynamic-update-slice_fusion.4
  146.7 2.2 maximum_dynamic-update-slice_fusion.5
  154.0 1.6 reshape.79
  157.1 1.6 reshape.78
  159.7 2.4 fusion.12
  162.8 2.2 maximum_dynamic-update-slice_fusion.4
  165.0 2.2 maximum_dynamic-update-slice_fusion.5
  178.1 2.4 fusion.12
  181.2 2.2 maximum_dynamic-update-slice_fusion.4
  183.4 2.2 maximum_dynamic-update-slice_fusion.5
  185.6 1.7 slice.48
  188.0 78.1 %pmax.15 = f32[4096]{0:T(1024)S(1)} all-reduce(f32[4096]{0:T(1024)S(1)} %slice.50), channel_id=1, replica_groups=mesh['rows'=32,'cols'=16] {'cols'}, use_global_device_ids=true, to_apply=%region_10.11 | all-reduce | flops 4096 | bytes 32768 | tf_op jit(solution)/shard_map/pmax | solution.py:92
  266.1 3.2 collective-permute-start.1
  269.3 100.7 %all-reduce.4.cloned.1.call-done = f32[65536]{0:T(1024)} async-done(((f32[65536]{0:T(1024)}), f32[65536]{0:T(1024)}) %all-reduce.4.cloned.1.call-update) | async-done | bytes 262160 | tf_op jit(solution)/shard_map/pmax | solution.py:92
  (214 shorter events, 45.3 us)
Async XLA Ops:
  6.5 32.3 %copy-start.3 = (s32[3,64]{1,0:T(4,128)S(1)}, s32[3,64]{1,0:T(4,128)}, u32[]{:S(2)}) copy-start(s32[3,64]{1,0:T(4,128)} %param.5) | copy-start | bytes 2308
  8.2 25.4 %all-to-all-start = ((f32[16,1,4096]{2,1,0:T(1,128)}), f32[16,1,4096]{2,1,0:T(1,128)S(1)}, u32[]{:S(2)}, u32[]{:S(2)}) async-start(f32[16,1,4096]{2,1,0:T(1,128)} %stack.2), calls=%async_computation | async-start | bytes 524288 | tf_op jit(solution)/shard_map/all_to_all | solution.py:64
  22.4 347.6 %all-reduce.4.cloned.1.call-start = ((), (), s32[]{:S(2)}) async-start(), calls=%async_computation.1 | async-start | bytes 524288 | tf_op jit(solution)/shard_map/pmax | solution.py:92
  33.6 4.5 %collective-permute-start = (f32[4096]{0:T(1024)S(1)}, f32[4096]{0:T(1024)S(1)}, u32[]{:S(2)}, u32[]{:S(2)}) collective-permute-start(f32[4096]{0:T(1024)S(1)} %bitcast.19), channel_id=1, source_target_pairs={{16,0},{32,16},{48,32},{64,48},{80,64},{96,80},{112,96},{128,112},... | collective-permute-start | bytes 49160 | tf_op jit(solution)/shard_map/ppermute | solution.py:19
  38.8 4.8 %copy-start.1 = (f32[69632]{0:T(1024)}, f32[69632]{0:T(1024)S(1)}, u32[]{:S(2)}) copy-start(f32[69632]{0:T(1024)S(1)} %get-tuple-element.293) | copy-start | bytes 835588 | tf_op jit(solution)/shard_map/while
  45.5 1.3 copy-start
  48.7 8.5 %copy-start.2 = (f32[69632]{0:T(1024)S(1)}, f32[69632]{0:T(1024)}, u32[]{:S(2)}) copy-start(f32[69632]{0:T(1024)} %copy-done.1) | copy-start | bytes 835588 | tf_op jit(solution)/shard_map/while
  57.2 4.8 %copy-start.1 = (f32[69632]{0:T(1024)}, f32[69632]{0:T(1024)S(1)}, u32[]{:S(2)}) copy-start(f32[69632]{0:T(1024)S(1)} %get-tuple-element.293) | copy-start | bytes 835588 | tf_op jit(solution)/shard_map/while
  63.9 1.3 copy-start
  67.0 8.5 %copy-start.2 = (f32[69632]{0:T(1024)S(1)}, f32[69632]{0:T(1024)}, u32[]{:S(2)}) copy-start(f32[69632]{0:T(1024)} %copy-done.1) | copy-start | bytes 835588 | tf_op jit(solution)/shard_map/while
  75.5 4.8 %copy-start.1 = (f32[69632]{0:T(1024)}, f32[69632]{0:T(1024)S(1)}, u32[]{:S(2)}) copy-start(f32[69632]{0:T(1024)S(1)} %get-tuple-element.293) | copy-start | bytes 835588 | tf_op jit(solution)/shard_map/while
  82.2 1.3 copy-start
  85.4 8.5 %copy-start.2 = (f32[69632]{0:T(1024)S(1)}, f32[69632]{0:T(1024)}, u32[]{:S(2)}) copy-start(f32[69632]{0:T(1024)} %copy-done.1) | copy-start | bytes 835588 | tf_op jit(solution)/shard_map/while
  93.8 4.8 %copy-start.1 = (f32[69632]{0:T(1024)}, f32[69632]{0:T(1024)S(1)}, u32[]{:S(2)}) copy-start(f32[69632]{0:T(1024)S(1)} %get-tuple-element.293) | copy-start | bytes 835588 | tf_op jit(solution)/shard_map/while
  100.5 1.3 copy-start
  103.7 8.5 %copy-start.2 = (f32[69632]{0:T(1024)S(1)}, f32[69632]{0:T(1024)}, u32[]{:S(2)}) copy-start(f32[69632]{0:T(1024)} %copy-done.1) | copy-start | bytes 835588 | tf_op jit(solution)/shard_map/while
  112.2 4.8 %copy-start.1 = (f32[69632]{0:T(1024)}, f32[69632]{0:T(1024)S(1)}, u32[]{:S(2)}) copy-start(f32[69632]{0:T(1024)S(1)} %get-tuple-element.293) | copy-start | bytes 835588 | tf_op jit(solution)/shard_map/while
  118.9 1.3 copy-start
  122.0 8.5 %copy-start.2 = (f32[69632]{0:T(1024)S(1)}, f32[69632]{0:T(1024)}, u32[]{:S(2)}) copy-start(f32[69632]{0:T(1024)} %copy-done.1) | copy-start | bytes 835588 | tf_op jit(solution)/shard_map/while
  130.5 4.8 %copy-start.1 = (f32[69632]{0:T(1024)}, f32[69632]{0:T(1024)S(1)}, u32[]{:S(2)}) copy-start(f32[69632]{0:T(1024)S(1)} %get-tuple-element.293) | copy-start | bytes 835588 | tf_op jit(solution)/shard_map/while
  137.2 1.3 copy-start
  140.4 8.5 %copy-start.2 = (f32[69632]{0:T(1024)S(1)}, f32[69632]{0:T(1024)}, u32[]{:S(2)}) copy-start(f32[69632]{0:T(1024)} %copy-done.1) | copy-start | bytes 835588 | tf_op jit(solution)/shard_map/while
  148.9 4.8 %copy-start.1 = (f32[69632]{0:T(1024)}, f32[69632]{0:T(1024)S(1)}, u32[]{:S(2)}) copy-start(f32[69632]{0:T(1024)S(1)} %get-tuple-element.293) | copy-start | bytes 835588 | tf_op jit(solution)/shard_map/while
  155.6 1.3 copy-start
  158.7 8.5 %copy-start.2 = (f32[69632]{0:T(1024)S(1)}, f32[69632]{0:T(1024)}, u32[]{:S(2)}) copy-start(f32[69632]{0:T(1024)} %copy-done.1) | copy-start | bytes 835588 | tf_op jit(solution)/shard_map/while
  167.2 4.8 %copy-start.1 = (f32[69632]{0:T(1024)}, f32[69632]{0:T(1024)S(1)}, u32[]{:S(2)}) copy-start(f32[69632]{0:T(1024)S(1)} %get-tuple-element.293) | copy-start | bytes 835588 | tf_op jit(solution)/shard_map/while
  173.9 1.3 copy-start
  177.1 8.5 %copy-start.2 = (f32[69632]{0:T(1024)S(1)}, f32[69632]{0:T(1024)}, u32[]{:S(2)}) copy-start(f32[69632]{0:T(1024)} %copy-done.1) | copy-start | bytes 835588 | tf_op jit(solution)/shard_map/while
  266.1 104.9 %collective-permute-start.1 = (f32[4096]{0:T(1024)S(1)}, f32[4096]{0:T(1024)S(1)}, u32[]{:S(2)}, u32[]{:S(2)}) collective-permute-start(f32[4096]{0:T(1024)S(1)} %pmax.15), channel_id=1, source_target_pairs={{0,16},{16,32},{32,48},{48,64},{64,80},{80,96},{96,112},{112,128},... | collective-permute-start | bytes 49160 | tf_op jit(solution)/shard_map/ppermute | solution.py:19
Sparse Core Ops, SparseCore 0:
  187.4 182.5 all-reduce.3
